TPU v7x, 512 devices: a whole 4x4x16 slice. The times are simulated.
512 devices in a mesh: gx: 8 (over z_lo), gy: 4 (over z_hi, core), gz: 16 (over y, x).
Axes of the slice: x: 4, y: 4, z: 16 (z_hi: 2, z_lo: 8; z = z_hi * 8 + z_lo), core: 2. Of those that a mesh axis runs over, the one named last changes fastest.
Arguments:
- probe_vectors: float32 [32, 16, 32, 2048], P(None, 'gx', 'gy', 'gz'), may hold values from -6 to 6
- layer_ids: int32 [16, 32, 2048], P('gx', 'gy', 'gz'), may hold values from 0 to 15
- layer_kappa: float32 [16], replicated, may hold values from 0.1 to 10
- slot_order: int32 [32, 16], replicated, may hold values from 0 to 511, as said below
Outputs:
- factored: float32 [16384, 16384], P(('gx', 'gy'), 'gz')
Inputs may be any that keep to these rules, and one draw needn't show every extreme that they name: `slot_order`: the entries are an ordering of 0 to 511, and in each column the entries divided by 16, rounded down, are an ordering of 0 to 31.
All inputs are finite; a program needn't handle non-finite values.
Results may differ from a plain program's by a relative error of at most 0.00013.
Values sent between devices are 32-bit elements; how exact they have to be, the bound alone decides.
No kernel may reach another device: no remote copies, remote signals or barrier semaphores. Data moves between devices by JAX's collectives and lax.ppermute only.
A program may use at most 128 MiB of HBM per device.

v0:
```python
import math
import jax
import jax.numpy as jnp
from jax import lax
from jax.sharding import PartitionSpec as P

PASSES = 4
PANEL = 256
NPAN = 2
upper_edge = 120.0
lower_edge = 24.0
coarse_shift = 1.0


def with_halo(block, sides, width):
    for axis, dim in sides:
        count = lax.axis_size(axis)
        forward = [(i, i + 1) for i in range(count - 1)]
        backward = [(target, source) for source, target in forward]
        low = lax.ppermute(
            lax.slice_in_dim(block, block.shape[dim] - width, None, axis=dim), axis, forward
        )
        high = lax.ppermute(lax.slice_in_dim(block, 0, width, axis=dim), axis, backward)
        block = jnp.concatenate([low, block, high], axis=dim)
    return block


def from_root(value, axis, source):
    kept = jnp.where(lax.axis_index(axis) == source, value, 0).astype(value.dtype)
    return lax.psum(kept, axis)


def cheb_factors(step_index):
    center = (upper_edge + lower_edge) / (upper_edge - lower_edge)
    growth = math.log(center + math.sqrt(center * center - 1.0))

    def chebval(degree):
        expo = math.exp(degree * growth)
        return 0.5 * (expo + 1.0 / expo)

    if step_index == 0:
        return (1.0 / chebval(1), 0.0)
    return (
        2.0 * chebval(step_index) / chebval(step_index + 1),
        chebval(step_index - 1) / chebval(step_index + 1),
    )


def face_weights(kappa_pad):
    center = kappa_pad[1:-1, 1:-1, 1:-1]
    x_plus = 0.5 * (center + kappa_pad[2:, 1:-1, 1:-1])
    x_minus = 0.5 * (center + kappa_pad[:-2, 1:-1, 1:-1])
    y_plus = 0.5 * (center + kappa_pad[1:-1, 2:, 1:-1])
    y_minus = 0.5 * (center + kappa_pad[1:-1, :-2, 1:-1])
    z_plus = 0.5 * (center + kappa_pad[1:-1, 1:-1, 2:])
    z_minus = 0.5 * (center + kappa_pad[1:-1, 1:-1, :-2])
    diagonal = x_plus + x_minus + y_plus + y_minus + z_plus + z_minus
    return ((x_plus, x_minus, y_plus, y_minus, z_plus, z_minus), diagonal)


def apply_operator(field_pad, weights, diagonal):
    x_plus, x_minus, y_plus, y_minus, z_plus, z_minus = weights
    interior = field_pad[..., 1:-1, 1:-1, 1:-1]
    beside = x_plus * field_pad[..., 2:, 1:-1, 1:-1] + x_minus * field_pad[..., :-2, 1:-1, 1:-1]
    beside = (
        beside + y_plus * field_pad[..., 1:-1, 2:, 1:-1] + y_minus * field_pad[..., 1:-1, :-2, 1:-1]
    )
    beside = (
        beside + z_plus * field_pad[..., 1:-1, 1:-1, 2:] + z_minus * field_pad[..., 1:-1, 1:-1, :-2]
    )
    return diagonal * interior - beside


def cheb_update(current, previous, applied, step_index):
    factor_one, factor_two = cheb_factors(step_index)
    shifted = (upper_edge + lower_edge) / (upper_edge - lower_edge) * current - 2.0 / (
        upper_edge - lower_edge
    ) * applied
    return factor_one * shifted - factor_two * previous


def face_block(own_face, weight_face, ghost_face, scaling):
    return -scaling * jnp.einsum(
        "kab,ab,lab->kl", own_face, weight_face, ghost_face, precision=lax.Precision.HIGHEST
    )


def table_lookup(table, row_wanted, col_wanted):
    row_ids = jnp.arange(table.shape[0], dtype=jnp.int32)
    col_ids = jnp.arange(table.shape[1], dtype=jnp.int32)
    hit = (row_wanted[..., None, None] == row_ids[:, None]) & (
        col_wanted[..., None, None] == col_ids[None, :]
    )
    return jnp.sum(jnp.where(hit, table, 0), axis=(-2, -1))


def on_device(probe_vectors, layer_ids, layer_kappa, slot_order):
    highest = lax.Precision.HIGHEST
    grid_x = lax.axis_size("gx")
    grid_y = lax.axis_size("gy")
    grid_z = lax.axis_size("gz")
    index_x = lax.axis_index("gx")
    index_y = lax.axis_index("gy")
    index_z = lax.axis_index("gz")
    vectors, extent_x, extent_y, extent_z = probe_vectors.shape
    layers = layer_kappa.shape[0]
    choose = layer_ids[None] == jnp.arange(layers, dtype=jnp.int32)[:, None, None, None]
    conductivity = jnp.sum(jnp.where(choose, layer_kappa[:, None, None, None], 0.0), axis=0)
    kappa_pad = with_halo(conductivity, (("gx", 0), ("gy", 1), ("gz", 2)), 1)
    weights, diagonal = face_weights(kappa_pad)
    current = probe_vectors
    previous = jnp.zeros_like(probe_vectors)
    for step_index in range(PASSES):
        padded = with_halo(current, (("gx", 1), ("gy", 2), ("gz", 3)), 1)
        applied = apply_operator(padded, weights, diagonal)
        current, previous = (cheb_update(current, previous, applied, step_index), current)
    ghosts = with_halo(current, (("gx", 1), ("gy", 2), ("gz", 3)), 1)
    local_image = apply_operator(
        jnp.pad(current, ((0, 0), (1, 1), (1, 1), (1, 1))), weights, diagonal
    )
    cell_count = extent_x * extent_y * extent_z
    scaling = 1.0 / math.sqrt(cell_count)
    flattened = current.reshape(vectors, cell_count)
    own_block = scaling * jnp.dot(
        flattened, local_image.reshape(vectors, cell_count).T, precision=highest
    )
    own_block = own_block + coarse_shift * jnp.eye(vectors, dtype=jnp.float32)
    x_plus, x_minus, y_plus, y_minus, z_plus, z_minus = weights
    blocks = jnp.stack(
        [
            own_block,
            face_block(current[:, 0], x_minus[0], ghosts[:, 0, 1:-1, 1:-1], scaling),
            face_block(current[:, -1], x_plus[-1], ghosts[:, -1, 1:-1, 1:-1], scaling),
            face_block(current[:, :, 0], y_minus[:, 0], ghosts[:, 1:-1, 0, 1:-1], scaling),
            face_block(current[:, :, -1], y_plus[:, -1], ghosts[:, 1:-1, -1, 1:-1], scaling),
            face_block(current[:, :, :, 0], z_minus[:, :, 0], ghosts[:, 1:-1, 1:-1, 0], scaling),
            face_block(current[:, :, :, -1], z_plus[:, :, -1], ghosts[:, 1:-1, 1:-1, -1], scaling),
        ]
    )
    rows_total = grid_x * grid_y
    row_index = index_x * grid_y + index_y
    row_ids = jnp.arange(rows_total, dtype=jnp.int32)
    group_of = slot_order // grid_z
    column_groups = lax.dynamic_index_in_dim(group_of, index_z, 1, keepdims=False)
    owner_source = jnp.sum(jnp.where(column_groups == row_index, row_ids, 0))
    piece = lax.all_gather(blocks[None], ("gx", "gy"), axis=0, tiled=True)
    anchor = jnp.arange(piece.shape[0], dtype=jnp.int32)
    wanted = (anchor == owner_source)[:, None, None, None]
    owned = jnp.sum(jnp.where(wanted, piece, 0.0), axis=0)
    sources = jnp.arange(grid_z, dtype=jnp.int32)
    source_rows = jnp.sum(jnp.where(group_of == row_index, row_ids[:, None], 0), axis=0)
    source_x = source_rows // grid_y
    source_y = source_rows % grid_y
    neighbour_rows = jnp.stack(
        [
            source_rows,
            source_rows - grid_y,
            source_rows + grid_y,
            source_rows - 1,
            source_rows + 1,
            source_rows,
            source_rows,
        ],
        axis=1,
    )
    neighbour_cols = jnp.stack(
        [sources, sources, sources, sources, sources, sources - 1, sources + 1], axis=1
    )
    always = jnp.ones((grid_z,), bool)
    usable = jnp.stack(
        [
            always,
            source_x > 0,
            source_x < grid_x - 1,
            source_y > 0,
            source_y < grid_y - 1,
            sources > 0,
            sources < grid_z - 1,
        ],
        axis=1,
    )
    targets = table_lookup(slot_order, neighbour_rows, neighbour_cols)
    own_slots = table_lookup(slot_order, source_rows, sources) - row_index * grid_z
    local_cols = targets - index_z * rows_total
    usable = usable & (local_cols >= 0) & (local_cols < rows_total)
    col_flat = jnp.where(usable, local_cols, rows_total).reshape(-1)
    row_flat = jnp.broadcast_to(own_slots[:, None], (grid_z, 7)).reshape(-1)
    empty_grid = jnp.zeros((grid_z, vectors, rows_total, vectors), jnp.float32)
    gathered = empty_grid.at[row_flat, :, col_flat, :].add(
        lax.all_gather(owned, "gz", axis=0, tiled=True), mode="drop"
    )
    coarse = gathered.reshape(grid_z * vectors, rows_total * vectors)
    rows_local = coarse.shape[0]
    cols_local = coarse.shape[1]
    panel_width = min(PANEL, rows_local, cols_local)
    global_rows = row_index * rows_local + jnp.arange(rows_local, dtype=jnp.int32)
    global_cols = index_z * cols_local + jnp.arange(cols_local, dtype=jnp.int32)
    offsets = jnp.arange(panel_width, dtype=jnp.int32)
    for panel_index in range(NPAN):
        panel_begin = panel_index * panel_width
        panel_end = panel_begin + panel_width
        row_root = panel_begin // rows_local
        col_root = panel_begin // cols_local
        row_start = panel_begin - row_root * rows_local
        col_start = panel_begin - col_root * cols_local
        column_piece = from_root(coarse[:, col_start : col_start + panel_width], "gz", col_root)
        row_piece, diagonal_piece = (
            from_root(coarse[row_start : row_start + panel_width, :], ("gx", "gy"), row_root),
            from_root(column_piece[row_start : row_start + panel_width, :], ("gx", "gy"), row_root),
        )
        factor = jnp.linalg.cholesky(diagonal_piece)
        row_factor = jax.scipy.linalg.solve_triangular(factor, column_piece.T, lower=True).T
        col_factor = jax.scipy.linalg.solve_triangular(factor, row_piece, lower=True).T
        row_factor = jnp.where(
            global_rows[:, None] >= panel_begin + offsets[None, :], row_factor, 0.0
        )
        updated = coarse - jnp.dot(row_factor, col_factor.T, precision=highest)
        trail_rows = global_rows >= panel_end
        trail_cols = global_cols >= panel_end
        panel_rows = (global_rows >= panel_begin) & (global_rows < panel_end)
        coarse = jnp.where(
            trail_rows[:, None] & trail_cols[None, :],
            updated,
            jnp.where(panel_rows[:, None] & trail_cols[None, :], 0.0, coarse),
        )
        old_columns = coarse[:, col_start : col_start + panel_width]
        new_columns = jnp.where(index_z == col_root, row_factor, old_columns)
        coarse = coarse.at[:, col_start : col_start + panel_width].set(new_columns)
    return coarse


def solution(mesh):
    in_specs = (P(None, "gx", "gy", "gz"), P("gx", "gy", "gz"), P(), P())
    out_specs = P(("gx", "gy"), "gz")
    return jax.shard_map(
        on_device, mesh=mesh, in_specs=in_specs, out_specs=out_specs, check_vma=False
    )
```

profile of v0, /device:TPU:1, one launch (start us, length us, event | category | flops | bytes accessed | tf_op | source)
XLA Modules:
  0.0 1363.8 jit_solution(13902177501467770364)
XLA Ops:
  8.7 5.0 collective-permute-start.1
  14.7 3.6 collective-permute-start.7
  20.8 3.0 select_reduce_fusion.1
  23.9 15.8 %collective-permute-start.3 = (f32[4,1,128]{2,1,0:T(1,128)S(1)}, f32[4,1,128]{2,1,0:T(1,128)S(1)}, u32[]{:S(2)}, u32[]{:S(2)}) collective-permute-start(f32[4,1,128]{2,1,0:T(1,128)S(1)} %get-tuple-element.143), channel_id=1, source_target_pairs={{0,16},{16,32},{32,48},{1,17},{17,33},{33,49},{2,18},{18,34},{34,5... | collective-permute-start | bytes 6152 | tf_op jit(solution)/shard_map/ppermute | solution.py:20
  41.7 11.6 collective-permute-done.2
  54.7 4.0 collective-permute-start.5
  62.7 12.4 collective-permute-start.9
  78.7 4.3 collective-permute-start.11
  85.8 4.8 collective-permute-start.13
  94.5 14.7 %collective-permute-start.15 = (f32[32,4,1,128]{3,0,2,1:T(8,128)S(1)}, f32[32,4,1,128]{3,0,2,1:T(8,128)S(1)}, u32[]{:S(2)}, u32[]{:S(2)}) collective-permute-start(f32[32,4,1,128]{3,0,2,1:T(8,128)S(1)} %get-tuple-element.117), channel_id=1, source_target_pairs={{0,16},{16,32},{32,48},{1,17},{17,33},{33,49},{2,18},{18,34},{34,5... | collective-permute-start | bytes 196616 | tf_op jit(solution)/shard_map/ppermute | solution.py:20
  113.1 4.6 collective-permute-start.17
  121.1 5.0 collective-permute-start.19
  130.0 14.2 %collective-permute-start.21 = (f32[32,4,1,128]{3,0,2,1:T(8,128)S(1)}, f32[32,4,1,128]{3,0,2,1:T(8,128)S(1)}, u32[]{:S(2)}, u32[]{:S(2)}) collective-permute-start(f32[32,4,1,128]{3,0,2,1:T(8,128)S(1)} %get-tuple-element.115), channel_id=1, source_target_pairs={{0,16},{16,32},{32,48},{1,17},{17,33},{33,49},{2,18},{18,34},{34,5... | collective-permute-start | bytes 196616 | tf_op jit(solution)/shard_map/ppermute | solution.py:20
  147.7 4.5 collective-permute-start.23
  155.2 4.7 collective-permute-start.25
  163.8 15.1 %collective-permute-start.27 = (f32[32,4,1,128]{3,0,2,1:T(8,128)S(1)}, f32[32,4,1,128]{3,0,2,1:T(8,128)S(1)}, u32[]{:S(2)}, u32[]{:S(2)}) collective-permute-start(f32[32,4,1,128]{3,0,2,1:T(8,128)S(1)} %get-tuple-element.113), channel_id=1, source_target_pairs={{0,16},{16,32},{32,48},{1,17},{17,33},{33,49},{2,18},{18,34},{34,5... | collective-permute-start | bytes 196616 | tf_op jit(solution)/shard_map/ppermute | solution.py:20
  182.4 4.9 collective-permute-start.29
  189.0 6.5 collective-permute-start.30
  197.7 6.0 collective-permute-done.31
  203.7 15.1 %collective-permute-start.32 = (f32[32,4,1,128]{3,0,2,1:T(8,128)S(1)}, f32[32,4,1,128]{3,0,2,1:T(8,128)S(1)}, u32[]{:S(2)}, u32[]{:S(2)}) collective-permute-start(f32[32,4,1,128]{3,0,2,1:T(8,128)S(1)} %get-tuple-element.112), channel_id=1, source_target_pairs={{0,16},{16,32},{32,48},{1,17},{17,33},{33,49},{2,18},{18,34},{34,5... | collective-permute-start | bytes 196616 | tf_op jit(solution)/shard_map/ppermute | solution.py:20
  221.5 12.0 collective-permute-done.33
  234.1 6.0 collective-permute-start.34
  242.3 5.3 collective-permute-done.35
  247.8 212.4 %all-gather = f32[224,32,32]{2,1,0:T(8,128)S(1)} all-gather(f32[7,32,32]{2,1,0:T(8,128)S(1)} %fusion.2), channel_id=2, replica_groups=mesh['gx'=8,'gy'=4,'gz'=16] {'gx','gy'}, dimensions={0}, use_global_device_ids=true | all-gather | bytes 946176 | tf_op jit(solution)/shard_map/all_gather | solution.py:146
  460.7 50.5 %all_gather.7 = f32[112,32,32]{2,1,0:T(8,128)S(1)} all-gather(f32[7,32,32]{2,1,0:T(8,128)S(1)} %select_reduce_fusion), channel_id=1, replica_groups=mesh['gx'=8,'gy'=4,'gz'=16] {'gz'}, dimensions={0}, use_global_device_ids=true | all-gather | bytes 487424 | tf_op jit(solution)/shard_map/all_gather | solution.py:190
  511.2 4.3 broadcast_in_dim.82
  515.5 16.4 %scatter_fusion = f32[16,32,32,32]{3,1,2,0:T(8,128)} fusion(f32[16,32,32,32]{3,1,2,0:T(8,128)} %broadcast_in_dim.82, s32[112]{0:T(128)S(1)} %fusion.191, f32[112,32,32]{2,1,0:T(8,128)S(1)} %all_gather.7), kind=kCustom, calls=%fused_computation | custom fusion | flops 114688 | bytes 1377152 | tf_op jit(solution)/shard_map/scatter-add | solution.py:189
  531.9 9.0 copy.208
  540.9 6.2 reshape.408
  548.2 3.0 slice_select_fusion
  551.2 4.3 copy.210
  555.5 4.6 select_n.194
  560.1 101.7 %all-reduce.9.cloned.1.call-done = f32[512,256]{0,1:T(8,128)} async-done(((f32[512,256]{0,1:T(8,128)}), f32[512,256]{0,1:T(8,128)}) %all-reduce.9.cloned.1.call-update) | async-done | bytes 524304 | tf_op jit(solution)/shard_map/psum | solution.py:30
  664.6 214.9 %all-reduce.15.cloned.1.call-done = (f32[256,1024]{1,0:T(8,128)}, f32[256,256]{0,1:T(8,128)}) async-done(((f32[256,1024]{1,0:T(8,128)}, f32[256,256]{0,1:T(8,128)}), (f32[256,1024]{1,0:T(8,128)}, f32[256,256]{0,1:T(8,128)})) %all-reduce.15.cloned.1.call-update) | async-done | bytes 1310736 | tf_op jit(solution)/shard_map/psum | solution.py:30
  881.6 11.7 cholesky.130
  893.3 9.8 custom-call.19
  903.6 11.7 cholesky.147
  918.2 4.0 while.10
  922.2 19.8 %custom-call.20 = f32[2,128,128]{1,2,0:T(8,128)S(1)} custom-call(f32[2,128,128]{2,1,0:T(8,128)S(1)} %get-tuple-element.60), custom_call_target="InvertDiagBlocksLowerTriangular" | custom-call | tf_op jit(solution)/shard_map/jit(_solve_triangular)/triangular_solve | solution.py:212
  950.6 113.2 %all-reduce.11.cloned.1.call-done = f32[512,256]{0,1:T(8,128)} async-done(((f32[512,256]{0,1:T(8,128)}), f32[512,256]{0,1:T(8,128)}) %all-reduce.11.cloned.1.call-update) | async-done | bytes 524304 | tf_op jit(solution)/shard_map/psum | solution.py:30
  1066.4 214.9 %all-reduce.13.cloned.1.call-done = (f32[256,1024]{0,1:T(8,128)}, f32[256,256]{0,1:T(8,128)}) async-done(((f32[256,1024]{0,1:T(8,128)}, f32[256,256]{0,1:T(8,128)}), (f32[256,1024]{0,1:T(8,128)}, f32[256,256]{0,1:T(8,128)})) %all-reduce.13.cloned.1.call-update) | async-done | bytes 1310736 | tf_op jit(solution)/shard_map/psum | solution.py:30
  1283.5 11.7 cholesky.164
  1295.2 9.8 custom-call.22
  1305.5 11.7 cholesky.181
  1319.9 4.0 while.11
  1323.9 19.9 %custom-call.23 = f32[2,128,128]{1,2,0:T(8,128)S(1)} custom-call(f32[2,128,128]{2,1,0:T(8,128)S(1)} %get-tuple-element.62), custom_call_target="InvertDiagBlocksLowerTriangular" | custom-call | tf_op jit(solution)/shard_map/jit(_solve_triangular)/triangular_solve | solution.py:212
  1347.4 3.9 select_select_fusion
  1354.0 2.9 copy.215
  (240 shorter events, 94.8 us)
Async XLA Ops:
  6.5 655.2 %all-reduce.9.cloned.1.call-start = ((), (), s32[]{:S(2)}) async-start(), calls=%async_computation | async-start | bytes 1048576 | tf_op jit(solution)/shard_map/psum | solution.py:30
  7.3 16.5 %collective-permute-start = (f32[1,8,128]{2,1,0:T(8,128)S(1)}, f32[1,8,128]{2,1,0:T(8,128)S(1)}, u32[]{:S(2)}, u32[]{:S(2)}) collective-permute-start(f32[1,8,128]{2,1,0:T(8,128)S(1)} %get-tuple-element.146), channel_id=1, source_target_pairs={{64,0},{128,64},{192,128},{256,192},{320,256},{384,320},{448,384},... | collective-permute-start | bytes 12296 | tf_op jit(solution)/shard_map/ppermute | solution.py:23
  8.7 15.2 %collective-permute-start.1 = (f32[1,8,128]{2,1,0:T(8,128)S(1)}, f32[1,8,128]{2,1,0:T(8,128)S(1)}, u32[]{:S(2)}, u32[]{:S(2)}) collective-permute-start(f32[1,8,128]{2,1,0:T(8,128)S(1)} %get-tuple-element.145), channel_id=1, source_target_pairs={{0,64},{64,128},{128,192},{192,256},{256,320},{320,384},{384,448},... | collective-permute-start | bytes 12296 | tf_op jit(solution)/shard_map/ppermute | solution.py:20
  14.7 45.0 %collective-permute-start.7 = (f32[32,1,8,128]{3,0,2,1:T(8,128)S(1)}, f32[32,1,8,128]{3,0,2,1:T(8,128)S(1)}, u32[]{:S(2)}, u32[]{:S(2)}) collective-permute-start(f32[32,1,8,128]{3,0,2,1:T(8,128)S(1)} %get-tuple-element.130), channel_id=1, source_target_pairs={{0,64},{64,128},{128,192},{192,256},{256,320},{320,384},{384,448},... | collective-permute-start | bytes 393224 | tf_op jit(solution)/shard_map/ppermute | solution.py:20
  18.3 42.5 %collective-permute-start.6 = (f32[32,1,8,128]{3,0,2,1:T(8,128)S(1)}, f32[32,1,8,128]{3,0,2,1:T(8,128)S(1)}, u32[]{:S(2)}, u32[]{:S(2)}) collective-permute-start(f32[32,1,8,128]{3,0,2,1:T(8,128)S(1)} %get-tuple-element.129), channel_id=1, source_target_pairs={{64,0},{128,64},{192,128},{256,192},{320,256},{384,320},{448,384},... | collective-permute-start | bytes 393224 | tf_op jit(solution)/shard_map/ppermute | solution.py:23
  23.9 17.7 %collective-permute-start.3 = (f32[4,1,128]{2,1,0:T(1,128)S(1)}, f32[4,1,128]{2,1,0:T(1,128)S(1)}, u32[]{:S(2)}, u32[]{:S(2)}) collective-permute-start(f32[4,1,128]{2,1,0:T(1,128)S(1)} %get-tuple-element.143), channel_id=1, source_target_pairs={{0,16},{16,32},{32,48},{1,17},{17,33},{33,49},{2,18},{18,34},{34,5... | collective-permute-start | bytes 6152 | tf_op jit(solution)/shard_map/ppermute | solution.py:20
  39.7 13.6 collective-permute-start.2
  53.4 5.4 collective-permute-start.4
  54.7 4.9 collective-permute-start.5
  60.8 14.4 %collective-permute-start.8 = (f32[32,4,1,128]{3,0,2,1:T(8,128)S(1)}, f32[32,4,1,128]{3,0,2,1:T(8,128)S(1)}, u32[]{:S(2)}, u32[]{:S(2)}) collective-permute-start(f32[32,4,1,128]{3,0,2,1:T(8,128)S(1)} %get-tuple-element.120), channel_id=1, source_target_pairs={{16,0},{32,16},{48,32},{17,1},{33,17},{49,33},{18,2},{34,18},{50,3... | collective-permute-start | bytes 196616 | tf_op jit(solution)/shard_map/ppermute | solution.py:23
  62.7 13.8 %collective-permute-start.9 = (f32[32,4,1,128]{3,0,2,1:T(8,128)S(1)}, f32[32,4,1,128]{3,0,2,1:T(8,128)S(1)}, u32[]{:S(2)}, u32[]{:S(2)}) collective-permute-start(f32[32,4,1,128]{3,0,2,1:T(8,128)S(1)} %get-tuple-element.119), channel_id=1, source_target_pairs={{0,16},{16,32},{32,48},{1,17},{17,33},{33,49},{2,18},{18,34},{34,5... | collective-permute-start | bytes 196616 | tf_op jit(solution)/shard_map/ppermute | solution.py:20
  77.1 5.9 collective-permute-start.10
  78.7 5.2 collective-permute-start.11
  83.3 7.4 copy-start.7
  84.5 6.6 collective-permute-start.12
  85.8 6.8 collective-permute-start.13
  92.6 16.8 %collective-permute-start.14 = (f32[32,4,1,128]{3,0,2,1:T(8,128)S(1)}, f32[32,4,1,128]{3,0,2,1:T(8,128)S(1)}, u32[]{:S(2)}, u32[]{:S(2)}) collective-permute-start(f32[32,4,1,128]{3,0,2,1:T(8,128)S(1)} %get-tuple-element.118), channel_id=1, source_target_pairs={{16,0},{32,16},{48,32},{17,1},{33,17},{49,33},{18,2},{34,18},{50,3... | collective-permute-start | bytes 196616 | tf_op jit(solution)/shard_map/ppermute | solution.py:23
  94.5 16.3 %collective-permute-start.15 = (f32[32,4,1,128]{3,0,2,1:T(8,128)S(1)}, f32[32,4,1,128]{3,0,2,1:T(8,128)S(1)}, u32[]{:S(2)}, u32[]{:S(2)}) collective-permute-start(f32[32,4,1,128]{3,0,2,1:T(8,128)S(1)} %get-tuple-element.117), channel_id=1, source_target_pairs={{0,16},{16,32},{32,48},{1,17},{17,33},{33,49},{2,18},{18,34},{34,5... | collective-permute-start | bytes 196616 | tf_op jit(solution)/shard_map/ppermute | solution.py:20
  110.9 8.5 copy-start.2
  111.5 7.3 collective-permute-start.16
  113.1 6.0 collective-permute-start.17
  119.8 6.7 collective-permute-start.18
  121.1 6.9 collective-permute-start.19
  128.1 16.8 %collective-permute-start.20 = (f32[32,4,1,128]{3,0,2,1:T(8,128)S(1)}, f32[32,4,1,128]{3,0,2,1:T(8,128)S(1)}, u32[]{:S(2)}, u32[]{:S(2)}) collective-permute-start(f32[32,4,1,128]{3,0,2,1:T(8,128)S(1)} %get-tuple-element.116), channel_id=1, source_target_pairs={{16,0},{32,16},{48,32},{17,1},{33,17},{49,33},{18,2},{34,18},{50,3... | collective-permute-start | bytes 196616 | tf_op jit(solution)/shard_map/ppermute | solution.py:23
  130.0 15.6 %collective-permute-start.21 = (f32[32,4,1,128]{3,0,2,1:T(8,128)S(1)}, f32[32,4,1,128]{3,0,2,1:T(8,128)S(1)}, u32[]{:S(2)}, u32[]{:S(2)}) collective-permute-start(f32[32,4,1,128]{3,0,2,1:T(8,128)S(1)} %get-tuple-element.115), channel_id=1, source_target_pairs={{0,16},{16,32},{32,48},{1,17},{17,33},{33,49},{2,18},{18,34},{34,5... | collective-permute-start | bytes 196616 | tf_op jit(solution)/shard_map/ppermute | solution.py:20
  146.1 6.2 collective-permute-start.22
  147.7 5.4 collective-permute-start.23
  153.9 6.5 collective-permute-start.24
  155.2 6.7 collective-permute-start.25
  161.9 17.2 %collective-permute-start.26 = (f32[32,4,1,128]{3,0,2,1:T(8,128)S(1)}, f32[32,4,1,128]{3,0,2,1:T(8,128)S(1)}, u32[]{:S(2)}, u32[]{:S(2)}) collective-permute-start(f32[32,4,1,128]{3,0,2,1:T(8,128)S(1)} %get-tuple-element.114), channel_id=1, source_target_pairs={{16,0},{32,16},{48,32},{17,1},{33,17},{49,33},{18,2},{34,18},{50,3... | collective-permute-start | bytes 196616 | tf_op jit(solution)/shard_map/ppermute | solution.py:23
  163.8 16.4 %collective-permute-start.27 = (f32[32,4,1,128]{3,0,2,1:T(8,128)S(1)}, f32[32,4,1,128]{3,0,2,1:T(8,128)S(1)}, u32[]{:S(2)}, u32[]{:S(2)}) collective-permute-start(f32[32,4,1,128]{3,0,2,1:T(8,128)S(1)} %get-tuple-element.113), channel_id=1, source_target_pairs={{0,16},{16,32},{32,48},{1,17},{17,33},{33,49},{2,18},{18,34},{34,5... | collective-permute-start | bytes 196616 | tf_op jit(solution)/shard_map/ppermute | solution.py:20
  180.8 6.7 collective-permute-start.28
  182.4 5.8 collective-permute-start.29
  189.0 8.7 collective-permute-start.30
  195.5 8.2 collective-permute-start.31
  203.7 17.8 %collective-permute-start.32 = (f32[32,4,1,128]{3,0,2,1:T(8,128)S(1)}, f32[32,4,1,128]{3,0,2,1:T(8,128)S(1)}, u32[]{:S(2)}, u32[]{:S(2)}) collective-permute-start(f32[32,4,1,128]{3,0,2,1:T(8,128)S(1)} %get-tuple-element.112), channel_id=1, source_target_pairs={{0,16},{16,32},{32,48},{1,17},{17,33},{33,49},{2,18},{18,34},{34,5... | collective-permute-start | bytes 196616 | tf_op jit(solution)/shard_map/ppermute | solution.py:20
  218.8 14.7 %collective-permute-start.33 = (f32[32,4,1,128]{3,0,2,1:T(8,128)S(1)}, f32[32,4,1,128]{3,0,2,1:T(8,128)S(1)}, u32[]{:S(2)}, u32[]{:S(2)}) collective-permute-start(f32[32,4,1,128]{3,0,2,1:T(8,128)S(1)} %get-tuple-element.111), channel_id=1, source_target_pairs={{16,0},{32,16},{48,32},{17,1},{33,17},{49,33},{18,2},{34,18},{50,3... | collective-permute-start | bytes 196616 | tf_op jit(solution)/shard_map/ppermute | solution.py:23
  234.1 8.0 collective-permute-start.34
  240.4 7.2 collective-permute-start.35
  547.2 4.0 copy-start
  548.1 331.4 %all-reduce.15.cloned.1.call-start = ((), (), s32[]{:S(2)}) async-start(), calls=%async_computation.3 | async-start | bytes 2621440 | tf_op jit(solution)/shard_map/psum | solution.py:30
  663.5 278.6 %copy-start.3 = (f32[512,256]{0,1:T(8,128)S(1)}, f32[512,256]{0,1:T(8,128)}, u32[]{:S(2)}) copy-start(f32[512,256]{0,1:T(8,128)} %all-reduce.9.cloned.1.call-done) | copy-start | bytes 1572868
  663.5 400.4 %all-reduce.11.cloned.1.call-start = ((), (), s32[]{:S(2)}) async-start(), calls=%async_computation.1 | async-start | bytes 1048576 | tf_op jit(solution)/shard_map/psum | solution.py:30
  903.2 40.1 %copy-start.5 = (f32[256,1024]{1,0:T(8,128)S(1)}, f32[256,1024]{1,0:T(8,128)}, u32[]{:S(2)}) copy-start(f32[256,1024]{1,0:T(8,128)} %get-tuple-element.84) | copy-start | bytes 3145732
  942.8 2.3 copy-start.1
  949.5 331.9 %all-reduce.13.cloned.1.call-start = ((), (), s32[]{:S(2)}) async-start(), calls=%async_computation.2 | async-start | bytes 2621440 | tf_op jit(solution)/shard_map/psum | solution.py:30
  1065.5 278.4 %copy-start.4 = (f32[512,256]{0,1:T(8,128)S(1)}, f32[512,256]{0,1:T(8,128)}, u32[]{:S(2)}) copy-start(f32[512,256]{0,1:T(8,128)} %all-reduce.11.cloned.1.call-done) | copy-start | bytes 1572868
  1343.9 1.3 copy-start.6
Sparse Core Ops, SparseCore 0:
  548.2 113.5 all-reduce.8
  664.2 215.2 all-reduce.14
  949.6 114.1 all-reduce.10
  1066.1 215.2 all-reduce.12
where the time goes:
time: 1370 us; the launch traced here: 1360 us
  waiting for transfers between devices  692 us (51%)
  blocking collectives  263 us (19%)
  starting transfers between devices  173 us (13%)
  other arithmetic  151 us (11%)
  local copies, waits for them, and re-layouts  51.9 us (4%)
  between operations  17.3 us (1%)
  matrix products  15.8 us (1%)
    psum x4, waiting for transfers between devices, from_root(): return lax.psum(kept, axis)  645 us
    all_gather x1, blocking collectives, on_device(): piece = lax.all_gather(blocks[None], ('gx', 'gy'), axis=0, tiled=True)  212 us
    ppermute x18, starting transfers between devices, with_halo(): lax.ppermute(lax.slice_in_dim(block, block.shape[dim] - width, None, axis...  145 us
    another operation x14, other arithmetic, on_device(): factor = jnp.linalg.cholesky(diagonal_piece)  69.3 us
    all_gather x1, blocking collectives, on_device(): lax.all_gather(owned, 'gz', axis=0, tiled=True)  50.5 us
    another operation x5, other arithmetic, on_device(): jax.scipy.linalg.solve_triangular(factor, column_piece.T, lower=True)  39.8 us
    ppermute x18, waiting for transfers between devices, with_halo(): lax.ppermute(lax.slice_in_dim(block, 0, width, axis=dim), axis, backward)  36 us
  transfers between devices with their start and end apart: 40, of which 24 were waited for; matrix products, arithmetic and copies ran while one was open for 2% of the time, Pallas kernels for 0%

commit v1 on v0

--- a/solution.py
+++ b/solution.py
@@ -143,7 +143,9 @@
     group_of = slot_order // grid_z
     column_groups = lax.dynamic_index_in_dim(group_of, index_z, 1, keepdims=False)
     owner_source = jnp.sum(jnp.where(column_groups == row_index, row_ids, 0))
-    piece = lax.all_gather(blocks[None], ("gx", "gy"), axis=0, tiled=True)
+    x = blocks[None]
+    outgoing = jnp.stack([x] * lax.axis_size(("gx", "gy")))
+    piece = jnp.concatenate(lax.all_to_all(outgoing, ("gx", "gy"), 0, 0), axis=0)
     anchor = jnp.arange(piece.shape[0], dtype=jnp.int32)
     wanted = (anchor == owner_source)[:, None, None, None]
     owned = jnp.sum(jnp.where(wanted, piece, 0.0), axis=0)

time: 1370 us -> 1210 us (0.88)
  blocking collectives: 263 us -> 30.6 us
  waiting for transfers between devices: 692 us -> 731 us
    all_gather x1 -> x0, blocking collectives: 212 us -> none  [on_device(): piece = lax.all_gather(blocks[None], ('gx', 'gy'), axis=0, tiled=True)]
    all_to_all x0 -> x1, waiting for transfers between devices: none -> 37.4 us  [on_device(): lax.all_to_all(outgoing, ('gx', 'gy'), 0, 0)]
    all_gather x1, blocking collectives: 50.5 us -> 30.6 us  [on_device(): lax.all_gather(owned, 'gz', axis=0, tiled=True)]
  transfers between devices with their start and end apart: 40 -> 41, of which waited for: 24 -> 27; matrix products, arithmetic and copies ran while one was open for 2% -> 2% of each run, Pallas kernels for 0% -> 0%
where the time goes in v1:
time: 1210 us; the launch traced here: 1190 us
  waiting for transfers between devices  731 us (60%)
  starting transfers between devices  183 us (15%)
  other arithmetic  154 us (13%)
  local copies, waits for them, and re-layouts  61.5 us (5%)
  blocking collectives  30.6 us (3%)
  between operations  17.4 us (1%)
  matrix products  15.8 us (1%)
    psum x4, waiting for transfers between devices, from_root(): return lax.psum(kept, axis)  646 us
    ppermute x18, starting transfers between devices, with_halo(): lax.ppermute(lax.slice_in_dim(block, block.shape[dim] - width, None, axis...  144 us
    another operation x14, other arithmetic, on_device(): factor = jnp.linalg.cholesky(diagonal_piece)  69.3 us
    another operation x5, other arithmetic, on_device(): jax.scipy.linalg.solve_triangular(factor, column_piece.T, lower=True)  39.8 us
    all_to_all x1, waiting for transfers between devices, on_device(): lax.all_to_all(outgoing, ('gx', 'gy'), 0, 0)  37.4 us
    ppermute x18, waiting for transfers between devices, with_halo(): lax.ppermute(lax.slice_in_dim(block, 0, width, axis=dim), axis, backward)  36.8 us
    all_gather x1, blocking collectives, on_device(): lax.all_gather(owned, 'gz', axis=0, tiled=True)  30.6 us
    ppermute x18, starting transfers between devices, with_halo(): lax.ppermute(lax.slice_in_dim(block, 0, width, axis=dim), axis, backward)  27 us
  transfers between devices with their start and end apart: 41, of which 27 were waited for; matrix products, arithmetic and copies ran while one was open for 2% of the time, Pallas kernels for 0%

profile of v1, /device:TPU:1, one launch (start us, length us, event | category | flops | bytes accessed | tf_op | source)
XLA Modules:
  0.0 1194.5 jit_solution(10513248559507528089)
XLA Ops:
  8.6 5.0 collective-permute-start.1
  14.7 16.6 %collective-permute-start.3 = (f32[4,1,128]{2,1,0:T(1,128)S(1)}, f32[4,1,128]{2,1,0:T(1,128)S(1)}, u32[]{:S(2)}, u32[]{:S(2)}) collective-permute-start(f32[4,1,128]{2,1,0:T(1,128)S(1)} %get-tuple-element.143), channel_id=1, source_target_pairs={{0,16},{16,32},{32,48},{1,17},{17,33},{33,49},{2,18},{18,34},{34,5... | collective-permute-start | bytes 6152 | tf_op jit(solution)/shard_map/ppermute | solution.py:20
  33.3 3.9 collective-permute-start.7
  37.3 7.7 collective-permute-done.2
  46.3 4.0 collective-permute-start.5
  52.8 3.8 collective-permute-done.6
  58.6 12.4 %collective-permute-start.9 = (f32[32,4,1,128]{3,0,2,1:T(8,128)S(1)}, f32[32,4,1,128]{3,0,2,1:T(8,128)S(1)}, u32[]{:S(2)}, u32[]{:S(2)}) collective-permute-start(f32[32,4,1,128]{3,0,2,1:T(8,128)S(1)} %get-tuple-element.119), channel_id=1, source_target_pairs={{0,16},{16,32},{32,48},{1,17},{17,33},{33,49},{2,18},{18,34},{34,5... | collective-permute-start | bytes 196616 | tf_op jit(solution)/shard_map/ppermute | solution.py:20
  74.5 4.0 collective-permute-start.11
  81.3 4.0 collective-permute-start.13
  89.2 15.6 %collective-permute-start.15 = (f32[32,4,1,128]{3,0,2,1:T(8,128)S(1)}, f32[32,4,1,128]{3,0,2,1:T(8,128)S(1)}, u32[]{:S(2)}, u32[]{:S(2)}) collective-permute-start(f32[32,4,1,128]{3,0,2,1:T(8,128)S(1)} %get-tuple-element.117), channel_id=1, source_target_pairs={{0,16},{16,32},{32,48},{1,17},{17,33},{33,49},{2,18},{18,34},{34,5... | collective-permute-start | bytes 196616 | tf_op jit(solution)/shard_map/ppermute | solution.py:20
  108.4 4.6 collective-permute-start.17
  115.9 4.7 collective-permute-start.19
  124.4 14.8 %collective-permute-start.21 = (f32[32,4,1,128]{3,0,2,1:T(8,128)S(1)}, f32[32,4,1,128]{3,0,2,1:T(8,128)S(1)}, u32[]{:S(2)}, u32[]{:S(2)}) collective-permute-start(f32[32,4,1,128]{3,0,2,1:T(8,128)S(1)} %get-tuple-element.115), channel_id=1, source_target_pairs={{0,16},{16,32},{32,48},{1,17},{17,33},{33,49},{2,18},{18,34},{34,5... | collective-permute-start | bytes 196616 | tf_op jit(solution)/shard_map/ppermute | solution.py:20
  142.8 4.6 collective-permute-start.23
  150.2 4.7 collective-permute-start.25
  158.8 15.0 %collective-permute-start.27 = (f32[32,4,1,128]{3,0,2,1:T(8,128)S(1)}, f32[32,4,1,128]{3,0,2,1:T(8,128)S(1)}, u32[]{:S(2)}, u32[]{:S(2)}) collective-permute-start(f32[32,4,1,128]{3,0,2,1:T(8,128)S(1)} %get-tuple-element.113), channel_id=1, source_target_pairs={{0,16},{16,32},{32,48},{1,17},{17,33},{33,49},{2,18},{18,34},{34,5... | collective-permute-start | bytes 196616 | tf_op jit(solution)/shard_map/ppermute | solution.py:20
  177.4 6.5 collective-permute-start.29
  185.5 4.1 collective-permute-start.30
  191.8 5.5 collective-permute-done.31
  197.2 16.1 %collective-permute-start.32 = (f32[32,4,1,128]{3,0,2,1:T(8,128)S(1)}, f32[32,4,1,128]{3,0,2,1:T(8,128)S(1)}, u32[]{:S(2)}, u32[]{:S(2)}) collective-permute-start(f32[32,4,1,128]{3,0,2,1:T(8,128)S(1)} %get-tuple-element.112), channel_id=1, source_target_pairs={{0,16},{16,32},{32,48},{1,17},{17,33},{33,49},{2,18},{18,34},{34,5... | collective-permute-start | bytes 196616 | tf_op jit(solution)/shard_map/ppermute | solution.py:20
  215.8 13.0 %collective-permute-done.33 = f32[32,4,1,128]{3,0,2,1:T(8,128)S(1)} collective-permute-done((f32[32,4,1,128]{3,0,2,1:T(8,128)S(1)}, f32[32,4,1,128]{3,0,2,1:T(8,128)S(1)}, u32[]{:S(2)}, u32[]{:S(2)}) %collective-permute-start.33) | collective-permute-done | bytes 65568 | tf_op jit(solution)/shard_map/ppermute | solution.py:23
  229.3 3.5 collective-permute-start.34
  235.1 5.3 collective-permute-done.35
  242.9 4.2 reshape.476
  247.1 11.6 all-to-all-start
  264.2 37.4 %all-to-all-done = f32[32,1,7168]{2,1,0:T(1,128)S(1)} async-done(((f32[32,1,7168]{2,1,0:T(1,128)}), f32[32,1,7168]{2,1,0:T(1,128)S(1)}, u32[]{:S(2)}, u32[]{:S(2)}) %all-to-all-start) | async-done | bytes 917536 | tf_op jit(solution)/shard_map/all_to_all | solution.py:148
  310.0 30.6 %all_gather.3 = f32[112,32,32]{2,1,0:T(8,128)S(1)} all-gather(f32[7,32,32]{2,1,0:T(8,128)S(1)} %fusion), channel_id=1, replica_groups=mesh['gx'=8,'gy'=4,'gz'=16] {'gz'}, dimensions={0}, use_global_device_ids=true | all-gather | bytes 487424 | tf_op jit(solution)/shard_map/all_gather | solution.py:192
  340.7 4.3 broadcast_in_dim.79
  345.0 16.4 %scatter_fusion = f32[16,32,32,32]{3,1,2,0:T(8,128)} fusion(f32[16,32,32,32]{3,1,2,0:T(8,128)} %broadcast_in_dim.79, s32[112]{0:T(128)S(1)} %fusion.192, f32[112,32,32]{2,1,0:T(8,128)S(1)} %all_gather.3), kind=kCustom, calls=%fused_computation | custom fusion | flops 114688 | bytes 1377152 | tf_op jit(solution)/shard_map/scatter-add | solution.py:191
  361.4 9.0 copy.208
  370.4 6.2 reshape.414
  380.7 4.3 copy.210
  385.0 4.6 select_n.194
  389.6 102.7 %all-reduce.9.cloned.1.call-done = f32[512,256]{0,1:T(8,128)} async-done(((f32[512,256]{0,1:T(8,128)}), f32[512,256]{0,1:T(8,128)}) %all-reduce.9.cloned.1.call-update) | async-done | bytes 524304 | tf_op jit(solution)/shard_map/psum | solution.py:30
  495.1 214.8 %all-reduce.15.cloned.1.call-done = (f32[256,1024]{1,0:T(8,128)}, f32[256,256]{0,1:T(8,128)}) async-done(((f32[256,1024]{1,0:T(8,128)}, f32[256,256]{0,1:T(8,128)}), (f32[256,1024]{1,0:T(8,128)}, f32[256,256]{0,1:T(8,128)})) %all-reduce.15.cloned.1.call-update) | async-done | bytes 1310736 | tf_op jit(solution)/shard_map/psum | solution.py:30
  712.0 11.7 cholesky.130
  723.8 9.8 custom-call.19
  734.1 11.7 cholesky.147
  748.6 4.2 while.10
  752.8 19.8 %custom-call.20 = f32[2,128,128]{1,2,0:T(8,128)S(1)} custom-call(f32[2,128,128]{2,1,0:T(8,128)S(1)} %get-tuple-element.60), custom_call_target="InvertDiagBlocksLowerTriangular" | custom-call | tf_op jit(solution)/shard_map/jit(_solve_triangular)/triangular_solve | solution.py:214
  781.3 113.2 %all-reduce.11.cloned.1.call-done = f32[512,256]{0,1:T(8,128)} async-done(((f32[512,256]{0,1:T(8,128)}), f32[512,256]{0,1:T(8,128)}) %all-reduce.11.cloned.1.call-update) | async-done | bytes 524304 | tf_op jit(solution)/shard_map/psum | solution.py:30
  897.1 215.0 %all-reduce.13.cloned.1.call-done = (f32[256,1024]{0,1:T(8,128)}, f32[256,256]{0,1:T(8,128)}) async-done(((f32[256,1024]{0,1:T(8,128)}, f32[256,256]{0,1:T(8,128)}), (f32[256,1024]{0,1:T(8,128)}, f32[256,256]{0,1:T(8,128)})) %all-reduce.13.cloned.1.call-update) | async-done | bytes 1310736 | tf_op jit(solution)/shard_map/psum | solution.py:30
  1114.1 11.7 cholesky.164
  1125.9 9.8 custom-call.22
  1136.2 11.7 cholesky.181
  1150.6 4.0 while.11
  1154.6 19.9 %custom-call.23 = f32[2,128,128]{1,2,0:T(8,128)S(1)} custom-call(f32[2,128,128]{2,1,0:T(8,128)S(1)} %get-tuple-element.62), custom_call_target="InvertDiagBlocksLowerTriangular" | custom-call | tf_op jit(solution)/shard_map/jit(_solve_triangular)/triangular_solve | solution.py:214
  1178.1 3.9 select_select_fusion
  (246 shorter events, 113.4 us)
Async XLA Ops:
  7.3 7.3 collective-permute-start
  8.6 6.0 collective-permute-start.1
  14.7 22.5 %collective-permute-start.3 = (f32[4,1,128]{2,1,0:T(1,128)S(1)}, f32[4,1,128]{2,1,0:T(1,128)S(1)}, u32[]{:S(2)}, u32[]{:S(2)}) collective-permute-start(f32[4,1,128]{2,1,0:T(1,128)S(1)} %get-tuple-element.143), channel_id=1, source_target_pairs={{0,16},{16,32},{32,48},{1,17},{17,33},{33,49},{2,18},{18,34},{34,5... | collective-permute-start | bytes 6152 | tf_op jit(solution)/shard_map/ppermute | solution.py:20
  31.3 13.6 %collective-permute-start.2 = (f32[4,1,128]{2,1,0:T(1,128)S(1)}, f32[4,1,128]{2,1,0:T(1,128)S(1)}, u32[]{:S(2)}, u32[]{:S(2)}) collective-permute-start(f32[4,1,128]{2,1,0:T(1,128)S(1)} %get-tuple-element.144), channel_id=1, source_target_pairs={{16,0},{32,16},{48,32},{17,1},{33,17},{49,33},{18,2},{34,18},{50,3... | collective-permute-start | bytes 6152 | tf_op jit(solution)/shard_map/ppermute | solution.py:23
  33.3 18.5 %collective-permute-start.7 = (f32[32,1,8,128]{3,0,2,1:T(8,128)S(1)}, f32[32,1,8,128]{3,0,2,1:T(8,128)S(1)}, u32[]{:S(2)}, u32[]{:S(2)}) collective-permute-start(f32[32,1,8,128]{3,0,2,1:T(8,128)S(1)} %get-tuple-element.130), channel_id=1, source_target_pairs={{0,64},{64,128},{128,192},{192,256},{256,320},{320,384},{384,448},... | collective-permute-start | bytes 393224 | tf_op jit(solution)/shard_map/ppermute | solution.py:20
  45.0 6.6 collective-permute-start.4
  46.3 5.3 collective-permute-start.5
  50.3 6.3 collective-permute-start.6
  56.6 14.5 %collective-permute-start.8 = (f32[32,4,1,128]{3,0,2,1:T(8,128)S(1)}, f32[32,4,1,128]{3,0,2,1:T(8,128)S(1)}, u32[]{:S(2)}, u32[]{:S(2)}) collective-permute-start(f32[32,4,1,128]{3,0,2,1:T(8,128)S(1)} %get-tuple-element.120), channel_id=1, source_target_pairs={{16,0},{32,16},{48,32},{17,1},{33,17},{49,33},{18,2},{34,18},{50,3... | collective-permute-start | bytes 196616 | tf_op jit(solution)/shard_map/ppermute | solution.py:23
  58.6 13.7 %collective-permute-start.9 = (f32[32,4,1,128]{3,0,2,1:T(8,128)S(1)}, f32[32,4,1,128]{3,0,2,1:T(8,128)S(1)}, u32[]{:S(2)}, u32[]{:S(2)}) collective-permute-start(f32[32,4,1,128]{3,0,2,1:T(8,128)S(1)} %get-tuple-element.119), channel_id=1, source_target_pairs={{0,16},{16,32},{32,48},{1,17},{17,33},{33,49},{2,18},{18,34},{34,5... | collective-permute-start | bytes 196616 | tf_op jit(solution)/shard_map/ppermute | solution.py:20
  72.9 5.6 collective-permute-start.10
  74.5 4.9 collective-permute-start.11
  80.0 5.7 collective-permute-start.12
  81.3 5.9 collective-permute-start.13
  87.3 17.5 %collective-permute-start.14 = (f32[32,4,1,128]{3,0,2,1:T(8,128)S(1)}, f32[32,4,1,128]{3,0,2,1:T(8,128)S(1)}, u32[]{:S(2)}, u32[]{:S(2)}) collective-permute-start(f32[32,4,1,128]{3,0,2,1:T(8,128)S(1)} %get-tuple-element.118), channel_id=1, source_target_pairs={{16,0},{32,16},{48,32},{17,1},{33,17},{49,33},{18,2},{34,18},{50,3... | collective-permute-start | bytes 196616 | tf_op jit(solution)/shard_map/ppermute | solution.py:23
  89.2 17.0 %collective-permute-start.15 = (f32[32,4,1,128]{3,0,2,1:T(8,128)S(1)}, f32[32,4,1,128]{3,0,2,1:T(8,128)S(1)}, u32[]{:S(2)}, u32[]{:S(2)}) collective-permute-start(f32[32,4,1,128]{3,0,2,1:T(8,128)S(1)} %get-tuple-element.117), channel_id=1, source_target_pairs={{0,16},{16,32},{32,48},{1,17},{17,33},{33,49},{2,18},{18,34},{34,5... | collective-permute-start | bytes 196616 | tf_op jit(solution)/shard_map/ppermute | solution.py:20
  106.2 7.9 copy-start.2
  106.8 6.2 collective-permute-start.16
  108.4 5.5 collective-permute-start.17
  114.6 6.4 collective-permute-start.18
  115.9 6.6 collective-permute-start.19
  122.5 16.9 %collective-permute-start.20 = (f32[32,4,1,128]{3,0,2,1:T(8,128)S(1)}, f32[32,4,1,128]{3,0,2,1:T(8,128)S(1)}, u32[]{:S(2)}, u32[]{:S(2)}) collective-permute-start(f32[32,4,1,128]{3,0,2,1:T(8,128)S(1)} %get-tuple-element.116), channel_id=1, source_target_pairs={{16,0},{32,16},{48,32},{17,1},{33,17},{49,33},{18,2},{34,18},{50,3... | collective-permute-start | bytes 196616 | tf_op jit(solution)/shard_map/ppermute | solution.py:23
  124.4 16.1 %collective-permute-start.21 = (f32[32,4,1,128]{3,0,2,1:T(8,128)S(1)}, f32[32,4,1,128]{3,0,2,1:T(8,128)S(1)}, u32[]{:S(2)}, u32[]{:S(2)}) collective-permute-start(f32[32,4,1,128]{3,0,2,1:T(8,128)S(1)} %get-tuple-element.115), channel_id=1, source_target_pairs={{0,16},{16,32},{32,48},{1,17},{17,33},{33,49},{2,18},{18,34},{34,5... | collective-permute-start | bytes 196616 | tf_op jit(solution)/shard_map/ppermute | solution.py:20
  141.2 6.2 collective-permute-start.22
  142.8 5.5 collective-permute-start.23
  148.9 6.4 collective-permute-start.24
  150.2 6.6 collective-permute-start.25
  156.9 17.1 %collective-permute-start.26 = (f32[32,4,1,128]{3,0,2,1:T(8,128)S(1)}, f32[32,4,1,128]{3,0,2,1:T(8,128)S(1)}, u32[]{:S(2)}, u32[]{:S(2)}) collective-permute-start(f32[32,4,1,128]{3,0,2,1:T(8,128)S(1)} %get-tuple-element.114), channel_id=1, source_target_pairs={{16,0},{32,16},{48,32},{17,1},{33,17},{49,33},{18,2},{34,18},{50,3... | collective-permute-start | bytes 196616 | tf_op jit(solution)/shard_map/ppermute | solution.py:23
  158.8 16.3 %collective-permute-start.27 = (f32[32,4,1,128]{3,0,2,1:T(8,128)S(1)}, f32[32,4,1,128]{3,0,2,1:T(8,128)S(1)}, u32[]{:S(2)}, u32[]{:S(2)}) collective-permute-start(f32[32,4,1,128]{3,0,2,1:T(8,128)S(1)} %get-tuple-element.113), channel_id=1, source_target_pairs={{0,16},{16,32},{32,48},{1,17},{17,33},{33,49},{2,18},{18,34},{34,5... | collective-permute-start | bytes 196616 | tf_op jit(solution)/shard_map/ppermute | solution.py:20
  175.8 8.3 collective-permute-start.28
  177.4 7.4 collective-permute-start.29
  185.5 6.2 collective-permute-start.30
  189.6 7.6 collective-permute-start.31
  197.2 18.5 %collective-permute-start.32 = (f32[32,4,1,128]{3,0,2,1:T(8,128)S(1)}, f32[32,4,1,128]{3,0,2,1:T(8,128)S(1)}, u32[]{:S(2)}, u32[]{:S(2)}) collective-permute-start(f32[32,4,1,128]{3,0,2,1:T(8,128)S(1)} %get-tuple-element.112), channel_id=1, source_target_pairs={{0,16},{16,32},{32,48},{1,17},{17,33},{33,49},{2,18},{18,34},{34,5... | collective-permute-start | bytes 196616 | tf_op jit(solution)/shard_map/ppermute | solution.py:20
  213.3 15.4 %collective-permute-start.33 = (f32[32,4,1,128]{3,0,2,1:T(8,128)S(1)}, f32[32,4,1,128]{3,0,2,1:T(8,128)S(1)}, u32[]{:S(2)}, u32[]{:S(2)}) collective-permute-start(f32[32,4,1,128]{3,0,2,1:T(8,128)S(1)} %get-tuple-element.111), channel_id=1, source_target_pairs={{16,0},{32,16},{48,32},{17,1},{33,17},{49,33},{18,2},{34,18},{50,3... | collective-permute-start | bytes 196616 | tf_op jit(solution)/shard_map/ppermute | solution.py:23
  229.3 5.5 collective-permute-start.34
  233.2 7.2 collective-permute-start.35
  242.9 16.0 %copy-start.7 = (s32[32,16]{0,1:T(8,128)S(1)}, s32[32,16]{0,1:T(8,128)}, u32[]{:S(2)}) copy-start(s32[32,16]{0,1:T(8,128)} %param.16) | copy-start | bytes 6148
  247.1 54.6 %all-to-all-start = ((f32[32,1,7168]{2,1,0:T(1,128)}), f32[32,1,7168]{2,1,0:T(1,128)S(1)}, u32[]{:S(2)}, u32[]{:S(2)}) async-start(f32[32,1,7168]{2,1,0:T(1,128)} %reshape.476), calls=%async_computation | async-start | bytes 1835008 | tf_op jit(solution)/shard_map/all_to_all | solution.py:148
  258.6 233.6 %all-reduce.9.cloned.1.call-start = ((), (), s32[]{:S(2)}) async-start(), calls=%async_computation.1 | async-start | bytes 1048576 | tf_op jit(solution)/shard_map/psum | solution.py:30
  376.6 4.0 copy-start
  377.6 332.4 %all-reduce.15.cloned.1.call-start = ((), (), s32[]{:S(2)}) async-start(), calls=%async_computation.4 | async-start | bytes 2621440 | tf_op jit(solution)/shard_map/psum | solution.py:30
  493.9 278.7 %copy-start.3 = (f32[512,256]{0,1:T(8,128)S(1)}, f32[512,256]{0,1:T(8,128)}, u32[]{:S(2)}) copy-start(f32[512,256]{0,1:T(8,128)} %all-reduce.9.cloned.1.call-done) | copy-start | bytes 1572868
  493.9 400.5 %all-reduce.11.cloned.1.call-start = ((), (), s32[]{:S(2)}) async-start(), calls=%async_computation.2 | async-start | bytes 1048576 | tf_op jit(solution)/shard_map/psum | solution.py:30
  733.6 40.3 %copy-start.5 = (f32[256,1024]{1,0:T(8,128)S(1)}, f32[256,1024]{1,0:T(8,128)}, u32[]{:S(2)}) copy-start(f32[256,1024]{1,0:T(8,128)} %get-tuple-element.84) | copy-start | bytes 3145732
  773.5 2.3 copy-start.1
  780.1 331.9 %all-reduce.13.cloned.1.call-start = ((), (), s32[]{:S(2)}) async-start(), calls=%async_computation.3 | async-start | bytes 2621440 | tf_op jit(solution)/shard_map/psum | solution.py:30
  896.2 278.4 %copy-start.4 = (f32[512,256]{0,1:T(8,128)S(1)}, f32[512,256]{0,1:T(8,128)}, u32[]{:S(2)}) copy-start(f32[512,256]{0,1:T(8,128)} %all-reduce.11.cloned.1.call-done) | copy-start | bytes 1572868
  (1 other events, 1.3 us)
Sparse Core Ops, SparseCore 0:
  377.7 114.5 all-reduce.8
  494.6 215.2 all-reduce.14
  780.3 114.1 all-reduce.10
  896.7 215.2 all-reduce.12
